TPU v7x, 32 devices: a whole 2x2x4 slice. The times are simulated.
32 devices in a mesh: patch: 4 (over y, x), uly: 8 (over z, core).
Axes of the slice: x: 2, y: 2, z: 4, core: 2. Of those that a mesh axis runs over, the one named last changes fastest.
Arguments:
- queries: bfloat16 [512, 3072], P(('patch', 'uly')), may hold values from -512 to 512
- keys_new: bfloat16 [512, 3072], P(('patch', 'uly')), may hold values from -6 to 6
- values_new: bfloat16 [512, 3072], P(('patch', 'uly')), may hold values from -6 to 6
- keys_old: bfloat16 [512, 3072], P(('patch', 'uly')), may hold values from -8 to 8
- values_old: bfloat16 [512, 3072], P(('patch', 'uly')), may hold values from -6 to 6
- gate_table: float32 [50, 3072], replicated, may hold values from 0.5 to 2
- step_index: int32 [1], replicated, may hold values from 0 to 49
Outputs:
- attended: bfloat16 [512, 3072], P(('patch', 'uly'))
All inputs are finite; a program needn't handle non-finite values.
Results may differ from a plain program's by a relative error of at most 0.0045.
Values may be sent and summed in bfloat16 or wider, within the bound.
No kernel may reach another device: no remote copies, remote signals or barrier semaphores. Data moves between devices by JAX's collectives and lax.ppermute only.
A program may use at most 64 MiB of HBM per device.

v0:
```python
import jax
import jax.numpy as jnp
from jax import lax
from jax.sharding import PartitionSpec as P

HEADS = 24
HEAD_DIM = 128


def absorb(carry, query_heads, key_piece, value_piece, masked):
    run_max, run_total, accumulated = carry
    score = jnp.einsum(
        "phd,khd->hpk", query_heads, key_piece, preferred_element_type=jnp.float32
    ) * HEAD_DIM ** (-0.5)
    score = jnp.where(masked[None, None, :], jnp.float32(-1e30), score)
    new_max = jnp.maximum(run_max, jnp.max(score, axis=-1))
    shrink = jnp.exp(run_max - new_max)
    expo = jnp.exp(score - new_max[..., None])
    run_total = run_total * shrink + jnp.sum(expo, axis=-1)
    update = jnp.einsum(
        "hpk,khd->phd", expo.astype(jnp.bfloat16), value_piece, preferred_element_type=jnp.float32
    )
    accumulated = accumulated * jnp.transpose(shrink)[..., None] + update
    return (new_max, run_total, accumulated)


def absorb_blocks(carry, query_heads, key_piece, value_piece, masked):
    count = key_piece.shape[0]
    span = 2048
    if count > span and count % span == 0:
        heads_here = key_piece.shape[1]
        key_blocks = key_piece.reshape(count // span, span, heads_here, HEAD_DIM)
        value_blocks = value_piece.reshape(count // span, span, heads_here, HEAD_DIM)
        mask_blocks = masked.reshape(count // span, span)

        def one_block(state, pieces):
            return (absorb(state, query_heads, pieces[0], pieces[1], pieces[2]), None)

        carry, unused = lax.scan(one_block, carry, (key_blocks, value_blocks, mask_blocks))
        return carry
    return absorb(carry, query_heads, key_piece, value_piece, masked)


def body(queries, keys_new, values_new, keys_old, values_old, gate_table, step_index):
    groups = lax.axis_size("uly")
    heads_here = HEADS // groups
    width_here = heads_here * HEAD_DIM
    patch_here = lax.axis_index("patch")
    fresh = (
        lax.all_to_all(queries, "uly", split_axis=1, concat_axis=0, tiled=True),
        lax.all_to_all(keys_new, "uly", split_axis=1, concat_axis=0, tiled=True),
        lax.all_to_all(values_new, "uly", split_axis=1, concat_axis=0, tiled=True),
    )
    query_heads = fresh[0].reshape(-1, heads_here, HEAD_DIM)
    fresh_keys = fresh[1].reshape(-1, heads_here, HEAD_DIM)
    fresh_values = fresh[2].reshape(-1, heads_here, HEAD_DIM)
    patch_rows = query_heads.shape[0]
    score = jnp.einsum(
        "phd,khd->hpk", query_heads, fresh_keys, preferred_element_type=jnp.float32
    ) * HEAD_DIM ** (-0.5)
    run_max = jnp.max(score, axis=-1)
    expo = jnp.exp(score - run_max[..., None])
    run_total = jnp.sum(expo, axis=-1)
    accumulated = jnp.einsum(
        "hpk,khd->phd", expo.astype(jnp.bfloat16), fresh_values, preferred_element_type=jnp.float32
    )
    carry = (run_max, run_total, accumulated)
    stale = (
        lax.all_to_all(keys_old, "uly", split_axis=1, concat_axis=0, tiled=True),
        lax.all_to_all(values_old, "uly", split_axis=1, concat_axis=0, tiled=True),
    )
    stale_keys = stale[0].reshape(-1, heads_here, HEAD_DIM)
    stale_values = stale[1].reshape(-1, heads_here, HEAD_DIM)
    pieces = (
        lax.all_gather(stale_keys, "patch", axis=0, tiled=True),
        lax.all_gather(stale_values, "patch", axis=0, tiled=True),
    )
    count = pieces[0].shape[0]
    masked = jnp.arange(count, dtype=jnp.int32) // patch_rows == patch_here
    carry = absorb_blocks(carry, query_heads, pieces[0], pieces[1], masked)
    run_max, run_total, accumulated = carry
    picker = (jnp.arange(gate_table.shape[0], dtype=jnp.int32) == step_index[0]).astype(jnp.float32)
    gate = jnp.dot(picker, gate_table, precision=lax.Precision.HIGHEST)
    gate_here = lax.dynamic_slice_in_dim(gate, lax.axis_index("uly") * width_here, width_here, 0)
    mixed = (accumulated / jnp.transpose(run_total)[..., None]).reshape(patch_rows, width_here)
    gated = (mixed * gate_here).astype(jnp.bfloat16)
    return lax.all_to_all(gated, "uly", split_axis=0, concat_axis=1, tiled=True)


def solution(mesh):
    in_specs = (
        P(("patch", "uly"), None),
        P(("patch", "uly"), None),
        P(("patch", "uly"), None),
        P(("patch", "uly"), None),
        P(("patch", "uly"), None),
        P(),
        P(),
    )
    out_specs = P(("patch", "uly"), None)
    return jax.shard_map(body, mesh=mesh, in_specs=in_specs, out_specs=out_specs, check_vma=False)
```

profile of v0, /device:TPU:0, one launch (start us, length us, event | category | flops | bytes accessed | tf_op | source)
XLA Modules:
  0.0 78.7 jit_solution(3090826867154986324)
XLA Ops:
  0.0 1.6 %copy.66 = bf16[2,8,8,384]{3,2,0,1:T(8,128)(2,1)} copy(bf16[2,8,8,384]{3,2,1,0:T(8,128)(2,1)} %bitcast.65) | data formatting | bytes 196608 | tf_op jit(solution)/shard_map/all_to_all | solution.py:50
  1.6 6.5 %all-to-all-start = ((bf16[16,8,384]{2,0,1:T(8,128)(2,1)}), bf16[16,8,384]{2,0,1:T(8,128)(2,1)S(1)}, u32[]{:S(2)}, u32[]{:S(2)}) async-start(bf16[16,8,384]{2,0,1:T(8,128)(2,1)} %bitcast.57), calls=%async_computation | async-start | bytes 196608 | tf_op jit(solution)/shard_map/all_to_all | solution.py:50
  8.1 0.7 copy.65
  8.8 5.7 %all-to-all-done = bf16[16,8,384]{2,0,1:T(8,128)(2,1)S(1)} async-done(((bf16[16,8,384]{2,0,1:T(8,128)(2,1)}), bf16[16,8,384]{2,0,1:T(8,128)(2,1)S(1)}, u32[]{:S(2)}, u32[]{:S(2)}) %all-to-all-start) | async-done | bytes 98336 | tf_op jit(solution)/shard_map/all_to_all | solution.py:50
  14.4 3.5 %all-to-all-start.1 = ((bf16[16,8,384]{2,0,1:T(8,128)(2,1)}), bf16[16,8,384]{2,0,1:T(8,128)(2,1)S(1)}, u32[]{:S(2)}, u32[]{:S(2)}) async-start(bf16[16,8,384]{2,0,1:T(8,128)(2,1)} %bitcast.56), calls=%async_computation.1 | async-start | bytes 196608 | tf_op jit(solution)/shard_map/all_to_all | solution.py:51
  17.9 0.6 copy.63
  19.2 4.9 %all-to-all-done.1 = bf16[16,8,384]{2,0,1:T(8,128)(2,1)S(1)} async-done(((bf16[16,8,384]{2,0,1:T(8,128)(2,1)}), bf16[16,8,384]{2,0,1:T(8,128)(2,1)S(1)}, u32[]{:S(2)}, u32[]{:S(2)}) %all-to-all-start.1) | async-done | bytes 98336 | tf_op jit(solution)/shard_map/all_to_all | solution.py:51
  24.2 3.4 %all-to-all-start.3 = ((bf16[16,8,384]{2,0,1:T(8,128)(2,1)}), bf16[16,8,384]{2,0,1:T(8,128)(2,1)S(1)}, u32[]{:S(2)}, u32[]{:S(2)}) async-start(bf16[16,8,384]{2,0,1:T(8,128)(2,1)} %bitcast.54), calls=%async_computation.3 | async-start | bytes 196608 | tf_op jit(solution)/shard_map/all_to_all | solution.py:69
  27.5 0.0 copy-start.3
  27.6 0.3 fusion.21
  27.9 0.5 copy-done.3
  28.4 0.7 copy.64
  29.1 0.3 copy-done.4
  29.4 0.6 copy.62
  30.0 0.1 dynamic_slice.3
  30.2 3.6 %all-to-all-done.3 = bf16[16,8,384]{2,0,1:T(8,128)(2,1)S(1)} async-done(((bf16[16,8,384]{2,0,1:T(8,128)(2,1)}), bf16[16,8,384]{2,0,1:T(8,128)(2,1)S(1)}, u32[]{:S(2)}, u32[]{:S(2)}) %all-to-all-start.3) | async-done | bytes 98336 | tf_op jit(solution)/shard_map/all_to_all | solution.py:69
  33.8 3.4 %all-to-all-start.2 = ((bf16[16,8,384]{2,0,1:T(8,128)(2,1)}), bf16[16,8,384]{2,0,1:T(8,128)(2,1)S(1)}, u32[]{:S(2)}, u32[]{:S(2)}) async-start(bf16[16,8,384]{2,0,1:T(8,128)(2,1)} %bitcast.55), calls=%async_computation.2 | async-start | bytes 196608 | tf_op jit(solution)/shard_map/all_to_all | solution.py:52
  37.2 9.5 %all_gather.6 = bf16[512,3,128]{2,0,1:T(8,128)(2,1)S(1)} all-gather(bf16[128,3,128]{2,0,1:T(8,128)(2,1)S(1)} %copy.30), channel_id=1, replica_groups=mesh['patch'=4,'uly'=8] {'patch'}, dimensions={0}, use_global_device_ids=true | all-gather | bytes 491520 | tf_op jit(solution)/shard_map/all_gather | solution.py:75
  46.7 0.4 fusion.28
  47.1 0.0 all-to-all-done.2
  47.1 5.0 %all-to-all-start.4 = ((bf16[16,8,384]{2,0,1:T(8,128)(2,1)}), bf16[16,8,384]{2,0,1:T(8,128)(2,1)S(1)}, u32[]{:S(2)}, u32[]{:S(2)}) async-start(bf16[16,8,384]{2,0,1:T(8,128)(2,1)} %bitcast.53), calls=%async_computation.4 | async-start | bytes 196608 | tf_op jit(solution)/shard_map/all_to_all | solution.py:70
  52.1 0.2 fusion.27
  52.4 0.1 fusion.8
  52.5 6.0 %all-to-all-done.4 = bf16[16,8,384]{2,0,1:T(8,128)(2,1)S(1)} async-done(((bf16[16,8,384]{2,0,1:T(8,128)(2,1)}), bf16[16,8,384]{2,0,1:T(8,128)(2,1)S(1)}, u32[]{:S(2)}, u32[]{:S(2)}) %all-to-all-start.4) | async-done | bytes 98336 | tf_op jit(solution)/shard_map/all_to_all | solution.py:70
  58.5 9.7 %all_gather.7 = bf16[512,3,128]{2,0,1:T(8,128)(2,1)S(1)} all-gather(bf16[128,3,128]{2,0,1:T(8,128)(2,1)S(1)} %copy.33), channel_id=1, replica_groups=mesh['patch'=4,'uly'=8] {'patch'}, dimensions={0}, use_global_device_ids=true | all-gather | bytes 491520 | tf_op jit(solution)/shard_map/all_gather | solution.py:76
  68.2 0.3 fusion.4
  68.5 0.2 fusion.3
  68.7 0.3 fusion.2
  69.1 0.1 copy.34
  69.2 0.1 reshape.75
  69.4 8.7 %all_to_all.96 = bf16[8,16,384]{2,1,0:T(8,128)(2,1)S(1)} all-to-all(bf16[8,16,384]{2,1,0:T(8,128)(2,1)S(1)} %multiply_convert_fusion), channel_id=1, replica_groups=mesh['patch'=4,'uly'=8] {'uly'}, dimensions={0} | all-to-all | bytes 196608 | tf_op jit(solution)/shard_map/all_to_all | solution.py:87
  78.1 0.7 copy.42
  (18 shorter events, 0.3 us)
Async XLA Ops:
  0.0 27.5 %copy-start = (f32[50,3072]{1,0:T(8,128)S(1)}, f32[50,3072]{1,0:T(8,128)}, u32[]{:S(2)}) copy-start(f32[50,3072]{1,0:T(8,128)} %param.12) | copy-start | bytes 1843204
  1.6 6.5 %copy-start.1 = (bf16[16,3072]{1,0:T(8,128)(2,1)S(1)}, bf16[16,3072]{1,0:T(8,128)(2,1)}, u32[]{:S(2)}) copy-start(bf16[16,3072]{1,0:T(8,128)(2,1)} %param.8) | copy-start | bytes 294916
  1.6 12.8 %all-to-all-start = ((bf16[16,8,384]{2,0,1:T(8,128)(2,1)}), bf16[16,8,384]{2,0,1:T(8,128)(2,1)S(1)}, u32[]{:S(2)}, u32[]{:S(2)}) async-start(bf16[16,8,384]{2,0,1:T(8,128)(2,1)} %bitcast.57), calls=%async_computation | async-start | bytes 196608 | tf_op jit(solution)/shard_map/all_to_all | solution.py:50
  14.4 3.5 %copy-start.2 = (bf16[16,3072]{1,0:T(8,128)(2,1)S(1)}, bf16[16,3072]{1,0:T(8,128)(2,1)}, u32[]{:S(2)}) copy-start(bf16[16,3072]{1,0:T(8,128)(2,1)} %param.10) | copy-start | bytes 294916
  14.4 9.7 %all-to-all-start.1 = ((bf16[16,8,384]{2,0,1:T(8,128)(2,1)}), bf16[16,8,384]{2,0,1:T(8,128)(2,1)S(1)}, u32[]{:S(2)}, u32[]{:S(2)}) async-start(bf16[16,8,384]{2,0,1:T(8,128)(2,1)} %bitcast.56), calls=%async_computation.1 | async-start | bytes 196608 | tf_op jit(solution)/shard_map/all_to_all | solution.py:51
  24.2 9.6 %all-to-all-start.3 = ((bf16[16,8,384]{2,0,1:T(8,128)(2,1)}), bf16[16,8,384]{2,0,1:T(8,128)(2,1)S(1)}, u32[]{:S(2)}, u32[]{:S(2)}) async-start(bf16[16,8,384]{2,0,1:T(8,128)(2,1)} %bitcast.54), calls=%async_computation.3 | async-start | bytes 196608 | tf_op jit(solution)/shard_map/all_to_all | solution.py:69
  27.5 0.9 %copy-start.3 = (bf16[16,3072]{1,0:T(8,128)(2,1)S(1)}, bf16[16,3072]{1,0:T(8,128)(2,1)}, u32[]{:S(2)}) copy-start(bf16[16,3072]{1,0:T(8,128)(2,1)} %param.9) | copy-start | bytes 294916
  28.4 0.9 %copy-start.4 = (bf16[16,3072]{1,0:T(8,128)(2,1)S(1)}, bf16[16,3072]{1,0:T(8,128)(2,1)}, u32[]{:S(2)}) copy-start(bf16[16,3072]{1,0:T(8,128)(2,1)} %param.11) | copy-start | bytes 294916
  33.8 13.3 %all-to-all-start.2 = ((bf16[16,8,384]{2,0,1:T(8,128)(2,1)}), bf16[16,8,384]{2,0,1:T(8,128)(2,1)S(1)}, u32[]{:S(2)}, u32[]{:S(2)}) async-start(bf16[16,8,384]{2,0,1:T(8,128)(2,1)} %bitcast.55), calls=%async_computation.2 | async-start | bytes 196608 | tf_op jit(solution)/shard_map/all_to_all | solution.py:52
  47.1 11.4 %all-to-all-start.4 = ((bf16[16,8,384]{2,0,1:T(8,128)(2,1)}), bf16[16,8,384]{2,0,1:T(8,128)(2,1)S(1)}, u32[]{:S(2)}, u32[]{:S(2)}) async-start(bf16[16,8,384]{2,0,1:T(8,128)(2,1)} %bitcast.53), calls=%async_computation.4 | async-start | bytes 196608 | tf_op jit(solution)/shard_map/all_to_all | solution.py:70
where the time goes:
time: 79.4 us; the launch traced here: 78.7 us
  blocking collectives  27.9 us (35%)
  starting transfers between devices  21.7 us (27%)
  waiting for transfers between devices  20.2 us (25%)
  local copies, waits for them, and re-layouts  6.2 us (8%)
  matrix products  1.49 us (2%)
  between operations  0.8 us (1%)
    all_gather x1, blocking collectives, body(): lax.all_gather(stale_values, 'patch', axis=0, tiled=True)  9.7 us
    all_gather x1, blocking collectives, body(): lax.all_gather(stale_keys, 'patch', axis=0, tiled=True)  9.52 us
    all_to_all x1, blocking collectives, body(): return lax.all_to_all(gated, 'uly', split_axis=0, concat_axis=1, tiled=True)  8.7 us
    all_to_all x1, starting transfers between devices, body(): lax.all_to_all(queries, 'uly', split_axis=1, concat_axis=0, tiled=True)  6.49 us
    all_to_all x1, waiting for transfers between devices, body(): lax.all_to_all(values_old, 'uly', split_axis=1, concat_axis=0, tiled=True)  5.98 us
    all_to_all x1, waiting for transfers between devices, body(): lax.all_to_all(queries, 'uly', split_axis=1, concat_axis=0, tiled=True)  5.65 us
    all_to_all x1, starting transfers between devices, body(): lax.all_to_all(values_old, 'uly', split_axis=1, concat_axis=0, tiled=True)  5.04 us
    all_to_all x1, waiting for transfers between devices, body(): lax.all_to_all(keys_new, 'uly', split_axis=1, concat_axis=0, tiled=True)  4.93 us
  transfers between devices with their start and end apart: 5, of which 4 were waited for; matrix products, arithmetic and copies ran while one was open for 5% of the time, Pallas kernels for 0%

commit v1 on v0

--- a/solution.py
+++ b/solution.py
@@ -5,6 +5,30 @@
 
 HEADS = 24
 HEAD_DIM = 128
+
+
+def split_up(x, dim, count):
+    shape = x.shape
+    pieces = x.reshape(*shape[:dim], count, shape[dim] // count, *shape[dim + 1 :])
+    return jnp.moveaxis(pieces, dim, 0)
+
+
+def joined_along(parts, dim):
+    parts = jnp.moveaxis(parts, 0, dim)
+    shape = parts.shape
+    return parts.reshape(*shape[:dim], shape[dim] * shape[dim + 1], *shape[dim + 2 :])
+
+
+def rotated_exchange(value, axis, split_dim, concat_dim):
+    size, index = (lax.axis_size(axis), lax.axis_index(axis))
+    tiles = split_up(value, split_dim, size)
+    result = tiles
+    for step in range(1, size):
+        target, source = ((index + step) % size, (index - step) % size)
+        sent = lax.dynamic_index_in_dim(tiles, target, 0)
+        partner_block = lax.ppermute(sent, axis, [(i, (i + step) % size) for i in range(size)])
+        result = lax.dynamic_update_slice_in_dim(result, partner_block, source, axis=0)
+    return joined_along(result, concat_dim)
 
 
 def absorb(carry, query_heads, key_piece, value_piece, masked):
@@ -67,7 +91,7 @@
     carry = (run_max, run_total, accumulated)
     stale = (
         lax.all_to_all(keys_old, "uly", split_axis=1, concat_axis=0, tiled=True),
-        lax.all_to_all(values_old, "uly", split_axis=1, concat_axis=0, tiled=True),
+        rotated_exchange(values_old, "uly", 1, 0),
     )
     stale_keys = stale[0].reshape(-1, heads_here, HEAD_DIM)
     stale_values = stale[1].reshape(-1, heads_here, HEAD_DIM)

time: 79.4 us -> 79.6 us (level)
  waiting for transfers between devices: 20.2 us -> 11.2 us
  starting transfers between devices: 21.7 us -> 27.2 us
  blocking collectives: 27.9 us -> 30.4 us
  local copies, waits for them, and re-layouts: 6.2 us -> 7.19 us
    ppermute x0 -> x7, starting transfers between devices: none -> 10.6 us  [rotated_exchange(): lax.ppermute(sent, axis, [(i, (i + step) % size) for i in range(size)])]
    all_to_all x1 -> x0, waiting for transfers between devices: 5.98 us -> none  [body(): lax.all_to_all(values_old, 'uly', split_axis=1, concat_axis=0, tiled=True)]
    all_to_all x1, waiting for transfers between devices: 5.65 us -> 0.01 us  [body(): lax.all_to_all(queries, 'uly', split_axis=1, concat_axis=0, tiled=True)]
    all_to_all x1 -> x0, starting transfers between devices: 5.04 us -> none  [body(): lax.all_to_all(values_old, 'uly', split_axis=1, concat_axis=0, tiled=True)]
    all_to_all x1, waiting for transfers between devices: 0.01 us -> 4.7 us  [body(): lax.all_to_all(values_new, 'uly', split_axis=1, concat_axis=0, tiled=True)]
    all_to_all x1, waiting for transfers between devices: 3.62 us -> 0.01 us  [body(): lax.all_to_all(keys_old, 'uly', split_axis=1, concat_axis=0, tiled=True)]
    all_to_all x1, starting transfers between devices: 6.49 us -> 3.36 us  [body(): lax.all_to_all(queries, 'uly', split_axis=1, concat_axis=0, tiled=True)]
    all_to_all x1, starting transfers between devices: 3.49 us -> 6.49 us  [body(): lax.all_to_all(keys_new, 'uly', split_axis=1, concat_axis=0, tiled=True)]
  transfers between devices with their start and end apart: 5 -> 11, of which waited for: 4 -> 4; matrix products, arithmetic and copies ran while one was open for 5% -> 5% of each run, Pallas kernels for 0% -> 0%
where the time goes in v1:
time: 79.6 us; the launch traced here: 79 us
  blocking collectives  30.4 us (38%)
  starting transfers between devices  27.2 us (34%)
  waiting for transfers between devices  11.2 us (14%)
  local copies, waits for them, and re-layouts  7.19 us (9%)
  matrix products  1.49 us (2%)
  between operations  1.17 us (1%)
    ppermute x7, starting transfers between devices, rotated_exchange(): lax.ppermute(sent, axis, [(i, (i + step) % size) for i in range(size)])  10.6 us
    all_to_all x1, blocking collectives, body(): return lax.all_to_all(gated, 'uly', split_axis=0, concat_axis=1, tiled=True)  10.5 us
    all_gather x1, blocking collectives, body(): lax.all_gather(stale_values, 'patch', axis=0, tiled=True)  10.2 us
    all_gather x1, blocking collectives, body(): lax.all_gather(stale_keys, 'patch', axis=0, tiled=True)  9.64 us
    all_to_all x1, starting transfers between devices, body(): lax.all_to_all(keys_new, 'uly', split_axis=1, concat_axis=0, tiled=True)  6.49 us
    all_to_all x1, waiting for transfers between devices, body(): lax.all_to_all(keys_new, 'uly', split_axis=1, concat_axis=0, tiled=True)  5.66 us
    all_to_all x1, waiting for transfers between devices, body(): lax.all_to_all(values_new, 'uly', split_axis=1, concat_axis=0, tiled=True)  4.7 us
    all_to_all x1, starting transfers between devices, body(): lax.all_to_all(values_new, 'uly', split_axis=1, concat_axis=0, tiled=True)  3.37 us
  transfers between devices with their start and end apart: 11, of which 4 were waited for; matrix products, arithmetic and copies ran while one was open for 5% of the time, Pallas kernels for 0%

profile of v1, /device:TPU:0, one launch (start us, length us, event | category | flops | bytes accessed | tf_op | source)
XLA Modules:
  0.0 79.0 jit_solution(2808541280268934694)
XLA Ops:
  0.0 1.6 %copy.81 = bf16[2,8,8,384]{3,2,0,1:T(8,128)(2,1)} copy(bf16[2,8,8,384]{3,2,1,0:T(8,128)(2,1)} %bitcast.79) | data formatting | bytes 196608 | tf_op jit(solution)/shard_map/all_to_all | solution.py:75
  1.6 6.5 %all-to-all-start.1 = ((bf16[16,8,384]{2,0,1:T(8,128)(2,1)}), bf16[16,8,384]{2,0,1:T(8,128)(2,1)S(1)}, u32[]{:S(2)}, u32[]{:S(2)}) async-start(bf16[16,8,384]{2,0,1:T(8,128)(2,1)} %bitcast.69), calls=%async_computation.1 | async-start | bytes 196608 | tf_op jit(solution)/shard_map/all_to_all | solution.py:75
  8.1 0.6 copy.82
  8.7 5.7 %all-to-all-done.1 = bf16[16,8,384]{2,0,1:T(8,128)(2,1)S(1)} async-done(((bf16[16,8,384]{2,0,1:T(8,128)(2,1)}), bf16[16,8,384]{2,0,1:T(8,128)(2,1)S(1)}, u32[]{:S(2)}, u32[]{:S(2)}) %all-to-all-start.1) | async-done | bytes 98336 | tf_op jit(solution)/shard_map/all_to_all | solution.py:75
  14.4 3.4 %all-to-all-start = ((bf16[16,8,384]{2,0,1:T(8,128)(2,1)}), bf16[16,8,384]{2,0,1:T(8,128)(2,1)S(1)}, u32[]{:S(2)}, u32[]{:S(2)}) async-start(bf16[16,8,384]{2,0,1:T(8,128)(2,1)} %bitcast.70), calls=%async_computation | async-start | bytes 196608 | tf_op jit(solution)/shard_map/all_to_all | solution.py:74
  17.9 0.8 %copy-done.2 = bf16[16,3072]{1,0:T(8,128)(2,1)S(1)} copy-done((bf16[16,3072]{1,0:T(8,128)(2,1)S(1)}, bf16[16,3072]{1,0:T(8,128)(2,1)}, u32[]{:S(2)}) %copy-start.2) | copy-done | bytes 98328
  18.7 0.2 dynamic-slice_bitcast_fusion
  18.9 0.4 collective-permute-start
  19.4 1.6 %collective-permute-start.1 = (bf16[1,16,384]{2,0,1:T(2,128)(2,1)S(1)}, bf16[1,16,384]{2,0,1:T(2,128)(2,1)S(1)}, u32[]{:S(2)}, u32[]{:S(2)}) collective-permute-start(bf16[1,16,384]{2,0,1:T(2,128)(2,1)S(1)} %get-tuple-element.12), channel_id=1, source_target_pairs={{0,2},{1,3},{2,4},{3,5},{4,6},{5,7},{6,0},{7,1},{8,10},{9,11},{10,... | collective-permute-start | bytes 36872 | tf_op jit(solution)/shard_map/ppermute | solution.py:29
  21.0 2.3 %collective-permute-start.2 = (bf16[1,16,384]{2,0,1:T(2,128)(2,1)S(1)}, bf16[1,16,384]{2,0,1:T(2,128)(2,1)S(1)}, u32[]{:S(2)}, u32[]{:S(2)}) collective-permute-start(bf16[1,16,384]{2,0,1:T(2,128)(2,1)S(1)} %get-tuple-element.11), channel_id=1, source_target_pairs={{0,3},{1,4},{2,5},{3,6},{4,7},{5,0},{6,1},{7,2},{8,11},{9,12},{10,... | collective-permute-start | bytes 36872 | tf_op jit(solution)/shard_map/ppermute | solution.py:29
  23.3 1.4 %collective-permute-start.3 = (bf16[1,16,384]{2,0,1:T(2,128)(2,1)S(1)}, bf16[1,16,384]{2,0,1:T(2,128)(2,1)S(1)}, u32[]{:S(2)}, u32[]{:S(2)}) collective-permute-start(bf16[1,16,384]{2,0,1:T(2,128)(2,1)S(1)} %get-tuple-element.10), channel_id=1, source_target_pairs={{0,4},{1,5},{2,6},{3,7},{4,0},{5,1},{6,2},{7,3},{8,12},{9,13},{10,... | collective-permute-start | bytes 36872 | tf_op jit(solution)/shard_map/ppermute | solution.py:29
  24.7 1.0 %collective-permute-start.4 = (bf16[1,16,384]{2,0,1:T(2,128)(2,1)S(1)}, bf16[1,16,384]{2,0,1:T(2,128)(2,1)S(1)}, u32[]{:S(2)}, u32[]{:S(2)}) collective-permute-start(bf16[1,16,384]{2,0,1:T(2,128)(2,1)S(1)} %get-tuple-element.9), channel_id=1, source_target_pairs={{0,5},{1,6},{2,7},{3,0},{4,1},{5,2},{6,3},{7,4},{8,13},{9,14},{10,... | collective-permute-start | bytes 36872 | tf_op jit(solution)/shard_map/ppermute | solution.py:29
  25.8 0.7 copy.80
  27.1 3.4 %all-to-all-start.2 = ((bf16[16,8,384]{2,0,1:T(8,128)(2,1)}), bf16[16,8,384]{2,0,1:T(8,128)(2,1)S(1)}, u32[]{:S(2)}, u32[]{:S(2)}) async-start(bf16[16,8,384]{2,0,1:T(8,128)(2,1)} %bitcast.68), calls=%async_computation.2 | async-start | bytes 196608 | tf_op jit(solution)/shard_map/all_to_all | solution.py:76
  30.5 0.3 fusion.21
  30.9 0.5 copy-done.4
  31.4 0.6 copy.79
  32.0 4.7 %all-to-all-done.2 = bf16[16,8,384]{2,0,1:T(8,128)(2,1)S(1)} async-done(((bf16[16,8,384]{2,0,1:T(8,128)(2,1)}), bf16[16,8,384]{2,0,1:T(8,128)(2,1)S(1)}, u32[]{:S(2)}, u32[]{:S(2)}) %all-to-all-start.2) | async-done | bytes 98336 | tf_op jit(solution)/shard_map/all_to_all | solution.py:76
  36.7 3.4 %all-to-all-start.3 = ((bf16[16,8,384]{2,0,1:T(8,128)(2,1)}), bf16[16,8,384]{2,0,1:T(8,128)(2,1)S(1)}, u32[]{:S(2)}, u32[]{:S(2)}) async-start(bf16[16,8,384]{2,0,1:T(8,128)(2,1)} %bitcast.67), calls=%async_computation.3 | async-start | bytes 196608 | tf_op jit(solution)/shard_map/all_to_all | solution.py:93
  40.1 3.7 %collective-permute-start.5 = (bf16[1,16,384]{2,0,1:T(2,128)(2,1)S(1)}, bf16[1,16,384]{2,0,1:T(2,128)(2,1)S(1)}, u32[]{:S(2)}, u32[]{:S(2)}) collective-permute-start(bf16[1,16,384]{2,0,1:T(2,128)(2,1)S(1)} %get-tuple-element.8), channel_id=1, source_target_pairs={{0,6},{1,7},{2,0},{3,1},{4,2},{5,3},{6,4},{7,5},{8,14},{9,15},{10,... | collective-permute-start | bytes 36872 | tf_op jit(solution)/shard_map/ppermute | solution.py:29
  44.7 0.7 collective-permute-done.5
  45.8 0.1 copy.49
  45.9 10.2 %all_gather.7 = bf16[512,3,128]{0,2,1:T(8,128)(2,1)S(1)} all-gather(bf16[128,3,128]{0,2,1:T(8,128)(2,1)S(1)} %copy.49), channel_id=1, replica_groups=mesh['patch'=4,'uly'=8] {'patch'}, dimensions={0}, use_global_device_ids=true | all-gather | bytes 491520 | tf_op jit(solution)/shard_map/all_gather | solution.py:100
  56.3 9.6 %all_gather.6 = bf16[512,3,128]{2,0,1:T(8,128)(2,1)S(1)} all-gather(bf16[128,3,128]{2,0,1:T(8,128)(2,1)S(1)} %copy.39), channel_id=1, replica_groups=mesh['patch'=4,'uly'=8] {'patch'}, dimensions={0}, use_global_device_ids=true | all-gather | bytes 491520 | tf_op jit(solution)/shard_map/all_gather | solution.py:99
  66.0 0.2 fusion.27
  66.2 0.4 fusion.28
  66.6 0.3 fusion.4
  66.9 0.2 fusion.3
  67.2 0.3 fusion.2
  67.5 0.1 copy.51
  67.8 10.5 %all_to_all.80 = bf16[8,16,384]{2,1,0:T(8,128)(2,1)S(1)} all-to-all(bf16[8,16,384]{2,1,0:T(8,128)(2,1)S(1)} %multiply_convert_fusion), channel_id=1, replica_groups=mesh['patch'=4,'uly'=8] {'uly'}, dimensions={0} | all-to-all | bytes 196608 | tf_op jit(solution)/shard_map/all_to_all | solution.py:111
  78.3 0.7 copy.59
  (39 shorter events, 1.4 us)
Async XLA Ops:
  0.0 30.5 %copy-start = (f32[50,3072]{1,0:T(8,128)S(1)}, f32[50,3072]{1,0:T(8,128)}, u32[]{:S(2)}) copy-start(f32[50,3072]{1,0:T(8,128)} %param.12) | copy-start | bytes 1843204
  1.6 6.5 %copy-start.1 = (bf16[16,3072]{1,0:T(8,128)(2,1)S(1)}, bf16[16,3072]{1,0:T(8,128)(2,1)}, u32[]{:S(2)}) copy-start(bf16[16,3072]{1,0:T(8,128)(2,1)} %param.7) | copy-start | bytes 294916
  1.6 12.8 %all-to-all-start.1 = ((bf16[16,8,384]{2,0,1:T(8,128)(2,1)}), bf16[16,8,384]{2,0,1:T(8,128)(2,1)S(1)}, u32[]{:S(2)}, u32[]{:S(2)}) async-start(bf16[16,8,384]{2,0,1:T(8,128)(2,1)} %bitcast.69), calls=%async_computation.1 | async-start | bytes 196608 | tf_op jit(solution)/shard_map/all_to_all | solution.py:75
  14.4 12.7 %all-to-all-start = ((bf16[16,8,384]{2,0,1:T(8,128)(2,1)}), bf16[16,8,384]{2,0,1:T(8,128)(2,1)S(1)}, u32[]{:S(2)}, u32[]{:S(2)}) async-start(bf16[16,8,384]{2,0,1:T(8,128)(2,1)} %bitcast.70), calls=%async_computation | async-start | bytes 196608 | tf_op jit(solution)/shard_map/all_to_all | solution.py:74
  17.8 0.9 %copy-start.2 = (bf16[16,3072]{1,0:T(8,128)(2,1)S(1)}, bf16[16,3072]{1,0:T(8,128)(2,1)}, u32[]{:S(2)}) copy-start(bf16[16,3072]{1,0:T(8,128)(2,1)} %param.11) | copy-start | bytes 294916
  18.7 7.1 %copy-start.3 = (bf16[16,3072]{1,0:T(8,128)(2,1)S(1)}, bf16[16,3072]{1,0:T(8,128)(2,1)}, u32[]{:S(2)}) copy-start(bf16[16,3072]{1,0:T(8,128)(2,1)} %param.9) | copy-start | bytes 294916
  18.9 21.2 %collective-permute-start = (bf16[1,16,384]{2,0,1:T(2,128)(2,1)S(1)}, bf16[1,16,384]{2,0,1:T(2,128)(2,1)S(1)}, u32[]{:S(2)}, u32[]{:S(2)}) collective-permute-start(bf16[1,16,384]{2,0,1:T(2,128)(2,1)S(1)} %get-tuple-element.13), channel_id=1, source_target_pairs={{0,1},{1,2},{2,3},{3,4},{4,5},{5,6},{6,7},{7,0},{8,9},{9,10},{10,1... | collective-permute-start | bytes 36872 | tf_op jit(solution)/shard_map/ppermute | solution.py:29
  19.4 24.5 %collective-permute-start.1 = (bf16[1,16,384]{2,0,1:T(2,128)(2,1)S(1)}, bf16[1,16,384]{2,0,1:T(2,128)(2,1)S(1)}, u32[]{:S(2)}, u32[]{:S(2)}) collective-permute-start(bf16[1,16,384]{2,0,1:T(2,128)(2,1)S(1)} %get-tuple-element.12), channel_id=1, source_target_pairs={{0,2},{1,3},{2,4},{3,5},{4,6},{5,7},{6,0},{7,1},{8,10},{9,11},{10,... | collective-permute-start | bytes 36872 | tf_op jit(solution)/shard_map/ppermute | solution.py:29
  21.0 23.3 %collective-permute-start.2 = (bf16[1,16,384]{2,0,1:T(2,128)(2,1)S(1)}, bf16[1,16,384]{2,0,1:T(2,128)(2,1)S(1)}, u32[]{:S(2)}, u32[]{:S(2)}) collective-permute-start(bf16[1,16,384]{2,0,1:T(2,128)(2,1)S(1)} %get-tuple-element.11), channel_id=1, source_target_pairs={{0,3},{1,4},{2,5},{3,6},{4,7},{5,0},{6,1},{7,2},{8,11},{9,12},{10,... | collective-permute-start | bytes 36872 | tf_op jit(solution)/shard_map/ppermute | solution.py:29
  23.3 21.2 %collective-permute-start.3 = (bf16[1,16,384]{2,0,1:T(2,128)(2,1)S(1)}, bf16[1,16,384]{2,0,1:T(2,128)(2,1)S(1)}, u32[]{:S(2)}, u32[]{:S(2)}) collective-permute-start(bf16[1,16,384]{2,0,1:T(2,128)(2,1)S(1)} %get-tuple-element.10), channel_id=1, source_target_pairs={{0,4},{1,5},{2,6},{3,7},{4,0},{5,1},{6,2},{7,3},{8,12},{9,13},{10,... | collective-permute-start | bytes 36872 | tf_op jit(solution)/shard_map/ppermute | solution.py:29
  24.7 19.9 %collective-permute-start.4 = (bf16[1,16,384]{2,0,1:T(2,128)(2,1)S(1)}, bf16[1,16,384]{2,0,1:T(2,128)(2,1)S(1)}, u32[]{:S(2)}, u32[]{:S(2)}) collective-permute-start(bf16[1,16,384]{2,0,1:T(2,128)(2,1)S(1)} %get-tuple-element.9), channel_id=1, source_target_pairs={{0,5},{1,6},{2,7},{3,0},{4,1},{5,2},{6,3},{7,4},{8,13},{9,14},{10,... | collective-permute-start | bytes 36872 | tf_op jit(solution)/shard_map/ppermute | solution.py:29
  27.1 9.6 %all-to-all-start.2 = ((bf16[16,8,384]{2,0,1:T(8,128)(2,1)}), bf16[16,8,384]{2,0,1:T(8,128)(2,1)S(1)}, u32[]{:S(2)}, u32[]{:S(2)}) async-start(bf16[16,8,384]{2,0,1:T(8,128)(2,1)} %bitcast.68), calls=%async_computation.2 | async-start | bytes 196608 | tf_op jit(solution)/shard_map/all_to_all | solution.py:76
  30.5 0.9 %copy-start.4 = (bf16[16,3072]{1,0:T(8,128)(2,1)S(1)}, bf16[16,3072]{1,0:T(8,128)(2,1)}, u32[]{:S(2)}) copy-start(bf16[16,3072]{1,0:T(8,128)(2,1)} %param.10) | copy-start | bytes 294916
  36.7 19.5 %all-to-all-start.3 = ((bf16[16,8,384]{2,0,1:T(8,128)(2,1)}), bf16[16,8,384]{2,0,1:T(8,128)(2,1)S(1)}, u32[]{:S(2)}, u32[]{:S(2)}) async-start(bf16[16,8,384]{2,0,1:T(8,128)(2,1)} %bitcast.67), calls=%async_computation.3 | async-start | bytes 196608 | tf_op jit(solution)/shard_map/all_to_all | solution.py:93
  40.1 5.3 %collective-permute-start.5 = (bf16[1,16,384]{2,0,1:T(2,128)(2,1)S(1)}, bf16[1,16,384]{2,0,1:T(2,128)(2,1)S(1)}, u32[]{:S(2)}, u32[]{:S(2)}) collective-permute-start(bf16[1,16,384]{2,0,1:T(2,128)(2,1)S(1)} %get-tuple-element.8), channel_id=1, source_target_pairs={{0,6},{1,7},{2,0},{3,1},{4,2},{5,3},{6,4},{7,5},{8,14},{9,15},{10,... | collective-permute-start | bytes 36872 | tf_op jit(solution)/shard_map/ppermute | solution.py:29
  43.9 1.7 %collective-permute-start.6 = (bf16[1,16,384]{2,0,1:T(2,128)(2,1)S(1)}, bf16[1,16,384]{2,0,1:T(2,128)(2,1)S(1)}, u32[]{:S(2)}, u32[]{:S(2)}) collective-permute-start(bf16[1,16,384]{2,0,1:T(2,128)(2,1)S(1)} %get-tuple-element.7), channel_id=1, source_target_pairs={{0,7},{1,0},{2,1},{3,2},{4,3},{5,4},{6,5},{7,6},{8,15},{9,8},{10,9... | collective-permute-start | bytes 36872 | tf_op jit(solution)/shard_map/ppermute | solution.py:29
